TPU v7x, 128 devices: a whole 4x4x4 slice. The times are simulated.
128 devices in a mesh: row: 16 (over y, x), col: 8 (over z, core).
Axes of the slice: x: 4, y: 4, z: 4, core: 2. Of those that a mesh axis runs over, the one named last changes fastest.
Arguments:
- row_emb: float32 [128, 300, 1024], P(('row', 'col')), may hold values from -1.5 to 1.5
- col_emb: float32 [128, 300, 1024], P(('row', 'col')), may hold values from -1.5 to 1.5
- row_acc: float32 [128, 300, 1024], P(('row', 'col')), may hold values from 0.5 to 8
- col_acc: float32 [128, 300, 1024], P(('row', 'col')), may hold values from 0.5 to 8
- marginal_log: float32 [131072], replicated, may hold values from -2 to 1
- tile_rows: int32 [384], P(('row', 'col')), may hold values from 0 to 127, as said below
- tile_cols: int32 [384], P(('row', 'col')), may hold values from 0 to 127, as said below
- counts: int32 [384, 1024, 1024], P(('row', 'col')), may hold values from 0 to 2047
Outputs:
- new_row_emb: float32 [128, 300, 1024], P(('row', 'col'))
- new_col_emb: float32 [128, 300, 1024], P(('row', 'col'))
- new_row_acc: float32 [128, 300, 1024], P(('row', 'col'))
- new_col_acc: float32 [128, 300, 1024], P(('row', 'col'))
Inputs may be any that keep to these rules, and one draw needn't show every extreme that they name: Block g of the embeddings lies on device g in the mesh's order (row slowest). Slot k lies on device p = k // 3; with p at row index r and col index c, tile_rows[k] // 8 equals r. With slot k on the device at col index c, tile_cols[k] % 8 equals c.
All inputs are finite; a program needn't handle non-finite values.
Results may differ from a plain program's by a relative error of at most 0.019.
Values may be sent and summed in bfloat16 or wider, within the bound.
No kernel may reach another device: no remote copies, remote signals or barrier semaphores. Data moves between devices by JAX's collectives and lax.ppermute only.
A program may use at most 128 MiB of HBM per device.

v0:
```python
import jax
import jax.numpy as jnp
from jax import lax
from jax.sharding import PartitionSpec as P

err_scale = 0.03125
learn_rate = 0.1


def split_up(array, dim, length):
    before, after = (array.shape[:dim], array.shape[dim + 1 :])
    return jnp.moveaxis(array.reshape(*before, length, -1, *after), dim, 0)


def sum_at_owner(array, axis, dim):
    length = lax.axis_size(axis)
    pieces = lax.all_to_all(split_up(array, dim, length), axis, 0, 0, tiled=True)
    return jnp.sum(pieces.astype(jnp.float32), axis=0)


def tile_terms(row_block, col_block, tile_counts, row_margin, col_margin):
    scores = lax.dot_general(
        row_block, col_block, (((0,), (0,)), ((), ())), preferred_element_type=jnp.float32
    )
    counted = tile_counts.astype(jnp.float32)
    shifted_log = jnp.log(jnp.maximum(counted, 1.0)) - row_margin[:, None] - col_margin[None, :]
    residue = scores - shifted_log
    weighted = (0.1 + 0.25 * jnp.sqrt(counted)) * residue
    cell_grad = jnp.where(tile_counts > 0, weighted, jax.nn.sigmoid(residue)) * err_scale
    errors = cell_grad.astype(jnp.bfloat16)
    row_term = lax.dot_general(
        col_block, errors, (((1,), (1,)), ((), ())), preferred_element_type=jnp.float32
    )
    col_term = jnp.dot(row_block, errors, preferred_element_type=jnp.float32)
    return (row_term, col_term)


def add_slot(buffer, slot_index, term):
    old_value = lax.dynamic_index_in_dim(buffer, slot_index, 0, keepdims=False)
    return lax.dynamic_update_index_in_dim(buffer, old_value + term, slot_index, 0)


def adagrad(weights, history, gradient):
    grown = history + gradient * gradient
    return (weights - learn_rate * gradient / jnp.sqrt(grown), grown)


def body(row_emb, col_emb, row_acc, col_acc, marginal_log, tile_rows, tile_cols, counts):
    col_count = lax.axis_size("col")
    row_count = lax.axis_size("row")
    emb_width = row_emb.shape[1]
    block_len = row_emb.shape[2]
    tile_total = counts.shape[0]
    row_low = row_emb.astype(jnp.bfloat16)
    col_low = col_emb.astype(jnp.bfloat16)
    rows_near = lax.all_gather(row_low, "col", axis=0, tiled=True)
    grads = (
        jnp.zeros((col_count, emb_width, block_len), jnp.float32),
        jnp.zeros((row_count, emb_width, block_len), jnp.float32),
    )
    cols_near = lax.all_gather(col_low, "row", axis=0, tiled=True)
    for tile_slot in range(tile_total):
        col_slot = tile_cols[tile_slot] // col_count
        col_block = lax.dynamic_index_in_dim(cols_near, col_slot, 0, keepdims=False)
        row_id = tile_rows[tile_slot]
        col_id = tile_cols[tile_slot]
        row_slot = row_id % col_count
        apply_col_slot = col_id // col_count
        row_block = lax.dynamic_index_in_dim(rows_near, row_slot, 0, keepdims=False)
        row_margin = lax.dynamic_slice_in_dim(marginal_log, row_id * block_len, block_len)
        col_margin = lax.dynamic_slice_in_dim(marginal_log, col_id * block_len, block_len)
        row_term, col_term = tile_terms(
            row_block, col_block, counts[tile_slot], row_margin, col_margin
        )
        grads = (
            add_slot(grads[0], row_slot, row_term),
            add_slot(grads[1], apply_col_slot, col_term),
        )
    row_sum = sum_at_owner(grads[0].astype(jnp.bfloat16), "col", 0)
    col_sum = lax.psum_scatter(
        grads[1].astype(jnp.bfloat16), "row", scatter_dimension=0, tiled=True
    ).astype(jnp.float32)
    new_row_emb, new_row_acc = adagrad(row_emb, row_acc, row_sum)
    new_col_emb, new_col_acc = adagrad(col_emb, col_acc, col_sum)
    return (new_row_emb, new_col_emb, new_row_acc, new_col_acc)


def solution(mesh):
    placed = (
        P(("row", "col"), None, None),
        P(("row", "col"), None, None),
        P(("row", "col"), None, None),
        P(("row", "col"), None, None),
        P(),
        P(("row", "col")),
        P(("row", "col")),
        P(("row", "col"), None, None),
    )
    return jax.shard_map(
        body,
        mesh=mesh,
        in_specs=placed,
        out_specs=(
            P(("row", "col"), None, None),
            P(("row", "col"), None, None),
            P(("row", "col"), None, None),
            P(("row", "col"), None, None),
        ),
        check_vma=False,
    )
```

profile of v0, /device:TPU:0, one launch (start us, length us, event | category | flops | bytes accessed | tf_op | source)
XLA Modules:
  0.0 274.2 jit_solution(9816080059861527763)
XLA Ops:
  7.2 0.0 copy-start.6
  7.2 0.0 copy-start.7
  7.2 0.0 all-gather.5.cloned.1.call-start
  7.2 2.3 copy.28
  9.5 0.0 all-gather.5.cloned.1.call-update
  9.6 0.0 all-gather.3.cloned.1.call-start
  9.6 2.3 copy.29
  11.9 0.0 all-gather.3.cloned.1.call-update
  11.9 0.0 reduce-scatter.4.cloned.1.call-start
  12.0 0.0 copy-done.6
  12.0 0.6 fusion.64
  20.0 0.0 copy-done.7
  20.0 0.6 fusion.63
  30.0 0.8 fusion.62
  30.8 17.6 %all-gather.5.cloned.1.call-done = bf16[8,300,1024]{2,1,0:T(8,128)(2,1)} async-done(((bf16[1,300,1024]{2,1,0:T(8,128)(2,1)}), bf16[8,300,1024]{2,1,0:T(8,128)(2,1)}) %all-gather.5.cloned.1.call-update) | async-done | bytes 4915216 | tf_op jit(solution)/shard_map/all_gather | solution.py:56
  48.3 80.5 %all-gather.3.cloned.1.call-done = bf16[16,300,1024]{2,1,0:T(8,128)(2,1)} async-done(((bf16[1,300,1024]{2,1,0:T(8,128)(2,1)}), bf16[16,300,1024]{2,1,0:T(8,128)(2,1)}) %all-gather.3.cloned.1.call-update) | async-done | bytes 9830416 | tf_op jit(solution)/shard_map/all_gather | solution.py:61
  128.8 8.2 %fusion.14 = bf16[1024,1024]{1,0:T(8,128)(2,1)} fusion(s32[3,1024,1024]{2,1,0:T(8,128)} %param.15, f32[1024]{0:T(1024)S(1)} %get-tuple-element.17, f32[1024]{0:T(1024)S(1)} %get-tuple-element.18, bf16[8,300,1024]{2,1,0:T(8,128)(2,1)} %all-gather.5.cloned.1.call-done, s32[]{:T(128)S(6)} %select_n.95, ...), kind=kOutput, calls=%fused_computation.22 | convolution fusion | flops 644874240 | bytes 7544840 | tf_op jit(solution)/shard_map/dot_general | solution.py:22
  137.0 9.2 %broadcast_in_dim.36 = f32[16,300,1024]{2,1,0:T(8,128)} broadcast(f32[]{:T(128)} %constant.108.clone.1), dimensions={} | broadcast | bytes 19660804 | tf_op jit(solution)/shard_map/broadcast_in_dim | solution.py:59
  146.2 0.0 copy-done.8
  146.2 3.0 %fusion.23 = f32[16,300,1024]{2,1,0:T(8,128)} fusion(f32[16,300,1024]{2,1,0:T(8,128)} %broadcast_in_dim.36, s32[]{:T(128)S(6)} %select_n.93, bf16[1024,1024]{1,0:T(8,128)(2,1)S(1)} %copy-done.8, bf16[8,300,1024]{2,1,0:T(8,128)(2,1)} %all-gather.5.cloned.1.call-done, s32[]{:T(128)S(6)} %select_n.95), kind=kOutput, calls=%fused_computation.38 | convolution fusion | flops 629145600 | bytes 3964936 | tf_op jit(solution)/shard_map/dot_general | solution.py:34
  149.2 1.5 constant_dynamic-slice_fusion.3
  150.7 0.0 slice-done.5
  150.7 0.0 slice-done.6
  150.8 0.0 slice-done.7
  150.8 0.0 slice-start.1
  150.8 0.0 slice-start.2
  150.8 0.0 slice-start.3
  150.8 0.0 slice-start.4
  150.8 5.6 %fusion.9 = bf16[1024,1024]{1,0:T(8,128)(2,1)S(1)} fusion(s32[3,1024,1024]{2,1,0:T(8,128)S(1)} %bitcast.136, f32[1024]{0:T(1024)S(1)} %get-tuple-element.15, f32[1024]{0:T(1024)S(1)} %get-tuple-element.16, bf16[8,300,1024]{2,1,0:T(8,128)(2,1)} %all-gather.5.cloned.1.call-done, s32[]{:T(128)S(6)} %select_n.100, ...), kind=kOutput, calls=%fused_computation.15 | convolution fusion | flops 644874240 | bytes 7544840 | tf_op jit(solution)/shard_map/dot_general | solution.py:22
  156.4 0.0 slice-done
  156.4 0.0 slice-done.1
  156.4 0.0 slice-done.2
  156.4 0.0 slice-done.3
  156.4 0.5 slice-done.4
  156.9 1.9 fusion.18
  158.8 0.1 constant_dynamic-slice_fusion.1
  159.0 5.6 %fusion.4 = bf16[1024,1024]{1,0:T(8,128)(2,1)S(1)} fusion(s32[3,1024,1024]{2,1,0:T(8,128)S(1)} %bitcast.136, f32[1024]{0:T(1024)S(1)} %get-tuple-element.19, f32[1024]{0:T(1024)S(1)} %get-tuple-element.14, bf16[8,300,1024]{2,1,0:T(8,128)(2,1)} %all-gather.5.cloned.1.call-done, s32[]{:T(128)S(6)} %select_n.107, ...), kind=kOutput, calls=%fused_computation.8 | convolution fusion | flops 644874240 | bytes 7544840 | tf_op jit(solution)/shard_map/dot_general | solution.py:22
  164.6 0.0 copy-start.2
  164.6 1.3 copy-done.2
  165.9 1.9 fusion.16
  167.8 5.0 %convert_element_type.49 = bf16[16,300,1024]{2,1,0:T(8,128)(2,1)} convert(f32[16,300,1024]{2,1,0:T(8,128)S(1)} %fusion.16) | non-fusion elementwise | flops 4915200 | bytes 29491200 | tf_op jit(solution)/shard_map/convert_element_type | solution.py:81
  172.8 0.0 reduce-scatter.4.cloned.1.call-update
  172.8 0.0 copy-start.9
  172.8 1.3 broadcast_in_dim.32
  174.1 0.3 copy-done.9
  174.4 1.9 fusion.24
  176.3 0.1 constant_dynamic-slice_fusion.2
  176.4 0.0 copy-start.3
  176.4 2.1 fusion.22
  178.5 0.1 constant_dynamic-slice_fusion
  178.6 0.0 copy-done.3
  178.6 1.9 fusion.20
  180.6 0.8 convert_bitcast_fusion
  181.4 62.3 %all_to_all.5 = bf16[8,1,300,1024]{3,2,1,0:T(8,128)(2,1)S(1)} all-to-all(bf16[8,1,300,1024]{3,2,1,0:T(8,128)(2,1)S(1)} %convert_bitcast_fusion), channel_id=1, replica_groups=mesh['row'=16,'col'=8] {'col'}, dimensions={0} | all-to-all | bytes 9830400 | tf_op jit(solution)/shard_map/all_to_all | solution.py:17
  243.7 1.1 convert_reduce_fusion
  244.9 0.4 multiply_bitcast_fusion
  245.2 0.0 copy-start.1
  245.2 0.0 copy-start.5
  245.2 0.5 copy-done.4
  245.8 5.8 %multiply_subtract_fusion = (f32[1,300,1024]{2,0,1:T(1,128)}, f32[1,300,1024]{2,0,1:T(1,128)}) fusion(f32[1,300,1024]{2,0,1:T(1,128)S(1)} %copy-done, f32[300,1024]{1,0:T(8,128)S(1)} %get-tuple-element.13, f32[1,300,1024]{2,0,1:T(1,128)S(1)} %copy-done.4, f32[1,300,1024]{2,1,0:T(8,128)S(1)} %get-tuple-element.12), kind=kLoop, calls=%fused_computation.47 | loop fusion | flops 921600 | bytes 7372800 | tf_op jit(solution)/shard_map/sub | solution.py:45
  251.6 9.8 %reduce-scatter.4.cloned.1.call-done = bf16[1,300,1024]{2,1,0:T(8,128)(2,1)} async-done(((bf16[16,300,1024]{2,1,0:T(8,128)(2,1)}), bf16[1,300,1024]{2,1,0:T(8,128)(2,1)}) %reduce-scatter.4.cloned.1.call-update) | async-done | bytes 614416
  261.4 1.8 fusion.26
  263.1 2.3 copy.21
  265.4 2.3 copy.22
  (12 shorter events, 0.0 us)
Async XLA Ops:
  7.2 4.8 %copy-start.6 = (s32[3]{0:T(128)S(1)}, s32[3]{0:T(128)}, u32[]{:S(2)}) copy-start(s32[3]{0:T(128)} %param.13) | copy-start | bytes 40
  7.2 12.9 %copy-start.7 = (s32[3]{0:T(128)S(1)}, s32[3]{0:T(128)}, u32[]{:S(2)}) copy-start(s32[3]{0:T(128)} %param.14) | copy-start | bytes 40
  7.2 41.2 %all-gather.5.cloned.1.call-start = ((), (), s32[]{:S(2)}) async-start(), calls=%async_computation.3 | async-start | bytes 5603328 | tf_op jit(solution)/shard_map/all_gather | solution.py:56
  9.6 119.3 %all-gather.3.cloned.1.call-start = ((), (), s32[]{:S(2)}) async-start(), calls=%async_computation.2 | async-start | bytes 10584064 | tf_op jit(solution)/shard_map/all_gather | solution.py:61
  11.9 249.4 %reduce-scatter.4.cloned.1.call-start = ((), (), s32[]{:S(2)}) async-start(), calls=%async_computation.4 | async-start | bytes 10584064
  128.8 21.9 %slice-start.5 = ((s8[12582912]{0:T(1024)(128)(4,1)}), s8[4194304]{0:T(1024)(128)(4,1)S(1)}, s32[]{:S(2)}) async-start(s8[12582912]{0:T(1024)(128)(4,1)} %bitcast.135), calls=%async_computation.10 | async-start | bytes 8388608
  128.8 21.9 %slice-start.6 = ((s8[12582912]{0:T(1024)(128)(4,1)}), s8[4194304]{0:T(1024)(128)(4,1)S(1)}, s32[]{:S(2)}) async-start(s8[12582912]{0:T(1024)(128)(4,1)} %bitcast.135), calls=%async_computation.11 | async-start | bytes 8388608
  137.0 9.3 %copy-start.8 = (bf16[1024,1024]{1,0:T(8,128)(2,1)S(1)}, bf16[1024,1024]{1,0:T(8,128)(2,1)}, u32[]{:S(2)}) copy-start(bf16[1024,1024]{1,0:T(8,128)(2,1)} %fusion.14) | copy-start | bytes 6291460
  137.0 13.8 %slice-start.7 = ((s8[12582912]{0:T(1024)(128)(4,1)}), s8[4194304]{0:T(1024)(128)(4,1)S(1)}, s32[]{:S(2)}) async-start(s8[12582912]{0:T(1024)(128)(4,1)} %bitcast.135), calls=%async_computation.12 | async-start | bytes 8388608
  149.2 7.2 %slice-start = ((s8[19922944]{0:T(1024)(128)(4,1)}), s8[4194304]{0:T(1024)(128)(4,1)S(1)}, s32[]{:S(2)}) async-start(s8[19922944]{0:T(1024)(128)(4,1)} %bitcast.133), calls=%async_computation.5 | async-start | bytes 8388608
  150.8 5.6 %slice-start.1 = ((s8[19922944]{0:T(1024)(128)(4,1)}), s8[4194304]{0:T(1024)(128)(4,1)S(1)}, s32[]{:S(2)}) async-start(s8[19922944]{0:T(1024)(128)(4,1)} %bitcast.133), calls=%async_computation.6 | async-start | bytes 8388608
  150.8 5.6 %slice-start.2 = ((s8[19922944]{0:T(1024)(128)(4,1)}), s8[4194304]{0:T(1024)(128)(4,1)S(1)}, s32[]{:S(2)}) async-start(s8[19922944]{0:T(1024)(128)(4,1)} %bitcast.133), calls=%async_computation.7 | async-start | bytes 8388608
  150.8 5.6 %slice-start.3 = ((s8[19922944]{0:T(1024)(128)(4,1)}), s8[4194304]{0:T(1024)(128)(4,1)S(1)}, s32[]{:S(2)}) async-start(s8[19922944]{0:T(1024)(128)(4,1)} %bitcast.133), calls=%async_computation.8 | async-start | bytes 8388608
  150.8 6.1 %slice-start.4 = ((s8[19922944]{0:T(1024)(128)(4,1)}), s8[3145728]{0:T(1024)(128)(4,1)S(1)}, s32[]{:S(2)}) async-start(s8[19922944]{0:T(1024)(128)(4,1)} %bitcast.133), calls=%async_computation.9 | async-start | bytes 6291456
  164.6 1.3 copy-start.2
  172.8 1.6 copy-start.9
  176.4 2.2 copy-start.3
  243.7 1.5 copy-start
  243.7 2.1 copy-start.4
  245.2 16.2 %copy-start.1 = (f32[1,300,1024]{2,0,1:T(1,128)S(1)}, f32[1,300,1024]{2,0,1:T(1,128)}, u32[]{:S(2)}) copy-start(f32[1,300,1024]{2,0,1:T(1,128)} %param.9) | copy-start | bytes 3686404
  245.2 16.1 %copy-start.5 = (f32[1,300,1024]{2,0,1:T(1,128)S(1)}, f32[1,300,1024]{2,0,1:T(1,128)}, u32[]{:S(2)}) copy-start(f32[1,300,1024]{2,0,1:T(1,128)} %param.11) | copy-start | bytes 3686404
Sparse Core Ops, SparseCore 0:
  10.3 38.0 all-gather.4
  51.0 77.7 all-gather.2
  172.9 88.4 reduce-scatter.3
where the time goes:
time: 275 us; the launch traced here: 274 us
  waiting for transfers between devices  108 us (39%)
  blocking collectives  62.3 us (23%)
  matrix products  32 us (12%)
  between operations  30.9 us (11%)
  local copies, waits for them, and re-layouts  26.2 us (10%)
  other arithmetic  14.8 us (5%)
    all_gather x1, waiting for transfers between devices, body(): cols_near = lax.all_gather(col_low, 'row', axis=0, tiled=True)  80.5 us
    all_to_all x1, blocking collectives, sum_at_owner(): lax.all_to_all(split_up(array, dim, length), axis, 0, 0, tiled=True)  62.3 us
    dot_general x3, matrix products, tile_terms(): lax.dot_general(row_block, col_block, (((0,), (0,)), ((), ())), preferred...  19.3 us
    all_gather x1, waiting for transfers between devices, body(): rows_near = lax.all_gather(row_low, 'col', axis=0, tiled=True)  17.6 us
    unnamed x40, local copies, waits for them, and re-layouts  11.9 us
    unnamed x4, waiting for transfers between devices  9.82 us
    broadcast_in_dim x1, local copies, waits for them, and re-layouts, body(): jnp.zeros((row_count, emb_width, block_len), jnp.float32)  9.25 us
    sub x2, other arithmetic, adagrad(): return (weights - learn_rate * gradient / jnp.sqrt(grown), grown)  7.58 us
  transfers between devices with their start and end apart: 3, of which 3 were waited for; matrix products, arithmetic and copies ran while one was open for 7% of the time, Pallas kernels for 0%

commit v1 on v0

--- a/solution.py
+++ b/solution.py
@@ -58,7 +58,8 @@
         jnp.zeros((col_count, emb_width, block_len), jnp.float32),
         jnp.zeros((row_count, emb_width, block_len), jnp.float32),
     )
-    cols_near = lax.all_gather(col_low, "row", axis=0, tiled=True)
+    stack = jnp.stack([col_low] * lax.axis_size("row"))
+    cols_near = jnp.concatenate(lax.all_to_all(stack, "row", 0, 0), axis=0)
     for tile_slot in range(tile_total):
         col_slot = tile_cols[tile_slot] // col_count
         col_block = lax.dynamic_index_in_dim(cols_near, col_slot, 0, keepdims=False)

time: 275 us -> 318 us (1.16)
  waiting for transfers between devices: 108 us -> 137 us
  starting transfers between devices: 0.12 us -> 7.59 us
    all_to_all x0 -> x1, waiting for transfers between devices: none -> 107 us  [body(): cols_near = jnp.concatenate(lax.all_to_all(stack, 'row', 0, 0), axis=0)]
    all_gather x1 -> x0, waiting for transfers between devices: 80.5 us -> none  [body(): cols_near = lax.all_gather(col_low, 'row', axis=0, tiled=True)]
    all_to_all x0 -> x1, starting transfers between devices: none -> 7.32 us  [body(): cols_near = jnp.concatenate(lax.all_to_all(stack, 'row', 0, 0), axis=0)]
    another operation x0 -> x1, local copies, waits for them, and re-layouts: none -> 5.1 us  [body(): stack = jnp.stack([col_low] * lax.axis_size('row'))]
    unnamed x40 -> x38, local copies, waits for them, and re-layouts: 11.9 us -> 7.98 us
    unnamed x4 -> x3, waiting for transfers between devices: 9.82 us -> 10.4 us
  transfers between devices with their start and end apart: 3 -> 3, of which waited for: 3 -> 3; matrix products, arithmetic and copies ran while one was open for 7% -> 6% of each run, Pallas kernels for 0% -> 0%
where the time goes in v1:
time: 318 us; the launch traced here: 317 us
  waiting for transfers between devices  137 us (43%)
  blocking collectives  63.2 us (20%)
  matrix products  32.1 us (10%)
  between operations  32 us (10%)
  local copies, waits for them, and re-layouts  27.4 us (9%)
  other arithmetic  17.5 us (6%)
  starting transfers between devices  7.59 us (2%)
    all_to_all x1, waiting for transfers between devices, body(): cols_near = jnp.concatenate(lax.all_to_all(stack, 'row', 0, 0), axis=0)  107 us
    all_to_all x1, blocking collectives, sum_at_owner(): lax.all_to_all(split_up(array, dim, length), axis, 0, 0, tiled=True)  63.2 us
    all_gather x1, waiting for transfers between devices, body(): rows_near = lax.all_gather(row_low, 'col', axis=0, tiled=True)  20.2 us
    dot_general x3, matrix products, tile_terms(): lax.dot_general(row_block, col_block, (((0,), (0,)), ((), ())), preferred...  19.4 us
    unnamed x3, waiting for transfers between devices  10.4 us
    broadcast_in_dim x1, local copies, waits for them, and re-layouts, body(): jnp.zeros((row_count, emb_width, block_len), jnp.float32)  9.26 us
    sub x2, other arithmetic, adagrad(): return (weights - learn_rate * gradient / jnp.sqrt(grown), grown)  8.14 us
    unnamed x38, local copies, waits for them, and re-layouts  7.98 us
  transfers between devices with their start and end apart: 3, of which 3 were waited for; matrix products, arithmetic and copies ran while one was open for 6% of the time, Pallas kernels for 0%

profile of v1, /device:TPU:0, one launch (start us, length us, event | category | flops | bytes accessed | tf_op | source)
XLA Modules:
  0.0 317.0 jit_solution(14954891264257005293)
XLA Ops:
  7.2 2.1 convert_element_type.41
  9.3 0.2 copy.31
  9.5 5.1 %stack.2 = bf16[16,1,300,1024]{3,2,1,0:T(8,128)(2,1)} broadcast(bf16[300,1024]{1,0:T(8,128)(2,1)S(1)} %bitcast.138), dimensions={2,3} | broadcast | bytes 10444800 | tf_op jit(solution)/shard_map/stack | solution.py:61
  14.6 7.3 %all-to-all-start = ((bf16[16,1,300,1024]{3,2,1,0:T(8,128)(2,1)}), bf16[16,1,300,1024]{3,2,1,0:T(8,128)(2,1)}, u32[]{:S(2)}, u32[]{:S(2)}) async-start(bf16[16,1,300,1024]{3,2,1,0:T(8,128)(2,1)} %stack.2), calls=%async_computation | async-start | bytes 19922944 | tf_op jit(solution)/shard_map/all_to_all | solution.py:62
  22.0 0.0 all-gather.2.cloned.1.call-start
  22.0 0.0 copy-done
  22.0 1.0 copy.28
  23.0 0.0 all-gather.2.cloned.1.call-update
  23.0 0.2 reduce-scatter.4.cloned.1.call-start
  23.3 0.0 copy-done.5
  23.3 0.6 fusion.64
  31.7 0.0 copy-done.6
  31.7 0.6 fusion.63
  42.1 0.8 fusion.62
  42.9 20.2 %all-gather.2.cloned.1.call-done = bf16[8,300,1024]{2,1,0:T(8,128)(2,1)} async-done(((bf16[1,300,1024]{2,1,0:T(8,128)(2,1)}), bf16[8,300,1024]{2,1,0:T(8,128)(2,1)}) %all-gather.2.cloned.1.call-update) | async-done | bytes 4915216 | tf_op jit(solution)/shard_map/all_gather | solution.py:56
  63.1 106.6 %all-to-all-done = bf16[16,1,300,1024]{3,2,1,0:T(8,128)(2,1)} async-done(((bf16[16,1,300,1024]{3,2,1,0:T(8,128)(2,1)}), bf16[16,1,300,1024]{3,2,1,0:T(8,128)(2,1)}, u32[]{:S(2)}, u32[]{:S(2)}) %all-to-all-start) | async-done | bytes 9830432 | tf_op jit(solution)/shard_map/all_to_all | solution.py:62
  169.7 8.2 %fusion.14 = bf16[1024,1024]{1,0:T(8,128)(2,1)} fusion(s32[3,1024,1024]{2,1,0:T(8,128)} %param.15, f32[1024]{0:T(1024)S(1)} %get-tuple-element.17, f32[1024]{0:T(1024)S(1)} %get-tuple-element.18, bf16[8,300,1024]{2,1,0:T(8,128)(2,1)} %all-gather.2.cloned.1.call-done, s32[]{:T(128)S(6)} %select_n.95, bf16[16,1,300,1024]{3,2,1,0:T(8,128)(2,1)} %all-to-all-done, ...), kind=kOutput, calls=%fused_computation.22 | convolution fusion | flops 644874240 | bytes 7544840 | tf_op jit(solution)/shard_map/dot_general | solution.py:22
  177.9 9.3 %broadcast_in_dim.36 = f32[16,300,1024]{2,1,0:T(8,128)} broadcast(f32[]{:T(128)} %constant.111.clone.1), dimensions={} | broadcast | bytes 19660804 | tf_op jit(solution)/shard_map/broadcast_in_dim | solution.py:59
  187.1 0.0 copy-done.7
  187.1 3.0 fusion.23
  190.1 1.5 constant_dynamic-slice_fusion.3
  191.6 0.0 slice-done.5
  191.6 0.0 slice-done.6
  191.7 0.0 slice-done.7
  191.7 0.0 slice-start.1
  191.7 0.0 slice-start.2
  191.7 0.0 slice-start.3
  191.7 0.0 slice-start.4
  191.7 5.6 %fusion.9 = bf16[1024,1024]{1,0:T(8,128)(2,1)S(1)} fusion(s32[3,1024,1024]{2,1,0:T(8,128)S(1)} %bitcast.140, f32[1024]{0:T(1024)S(1)} %get-tuple-element.15, f32[1024]{0:T(1024)S(1)} %get-tuple-element.16, bf16[8,300,1024]{2,1,0:T(8,128)(2,1)} %all-gather.2.cloned.1.call-done, s32[]{:T(128)S(6)} %select_n.100, bf16[16,1,300,1024]{3,2,1,0:T(8,128)(2,1)} %all-to-all-done, ...), kind=kOutput, calls=%fused_computation.15 | convolution fusion | flops 644874240 | bytes 7544840 | tf_op jit(solution)/shard_map/dot_general | solution.py:22
  197.3 0.0 slice-done
  197.3 0.0 slice-done.1
  197.3 0.0 slice-done.2
  197.3 0.0 slice-done.3
  197.3 0.5 slice-done.4
  197.8 1.9 fusion.18
  199.7 0.1 constant_dynamic-slice_fusion.1
  199.9 5.6 %fusion.4 = bf16[1024,1024]{1,0:T(8,128)(2,1)S(1)} fusion(s32[3,1024,1024]{2,1,0:T(8,128)S(1)} %bitcast.140, f32[1024]{0:T(1024)S(1)} %get-tuple-element.19, f32[1024]{0:T(1024)S(1)} %get-tuple-element.14, bf16[8,300,1024]{2,1,0:T(8,128)(2,1)} %all-gather.2.cloned.1.call-done, s32[]{:T(128)S(6)} %select_n.107, bf16[16,1,300,1024]{3,2,1,0:T(8,128)(2,1)} %all-to-all-done, ...), kind=kOutput, calls=%fused_computation.8 | convolution fusion | flops 644874240 | bytes 7544840 | tf_op jit(solution)/shard_map/dot_general | solution.py:22
  205.5 0.0 copy-start.2
  205.5 1.3 copy-done.2
  206.8 1.9 fusion.16
  208.7 5.0 %convert_element_type.52 = bf16[16,300,1024]{2,1,0:T(8,128)(2,1)} convert(f32[16,300,1024]{2,1,0:T(8,128)S(1)} %fusion.16) | non-fusion elementwise | flops 4915200 | bytes 29491200 | tf_op jit(solution)/shard_map/convert_element_type | solution.py:82
  213.7 0.0 reduce-scatter.4.cloned.1.call-update
  213.7 0.0 copy-start.8
  213.8 1.3 broadcast_in_dim.32
  215.0 0.3 copy-done.8
  215.3 1.9 fusion.24
  217.3 0.1 constant_dynamic-slice_fusion.2
  217.4 0.0 copy-start.3
  217.4 2.1 fusion.22
  219.5 0.1 constant_dynamic-slice_fusion
  219.6 0.0 copy-done.3
  219.6 1.9 fusion.20
  221.5 0.8 convert_bitcast_fusion
  222.3 63.2 %all_to_all.10 = bf16[8,1,300,1024]{3,2,1,0:T(8,128)(2,1)S(1)} all-to-all(bf16[8,1,300,1024]{3,2,1,0:T(8,128)(2,1)S(1)} %convert_bitcast_fusion), channel_id=1, replica_groups=mesh['row'=16,'col'=8] {'col'}, dimensions={0} | all-to-all | bytes 9830400 | tf_op jit(solution)/shard_map/all_to_all | solution.py:17
  285.5 1.1 convert_reduce_fusion
  286.7 0.3 multiply_bitcast_fusion
  287.0 0.0 copy-start.1
  287.0 0.0 copy-done.4
  287.0 6.0 %multiply_subtract_fusion = (f32[1,300,1024]{2,0,1:T(1,128)}, f32[1,300,1024]{2,0,1:T(1,128)}) fusion(f32[1,300,1024]{2,0,1:T(1,128)S(1)} %copy-done, f32[300,1024]{1,0:T(8,128)S(1)} %get-tuple-element.13, f32[1,300,1024]{2,0,1:T(1,128)S(1)} %copy-done.4, f32[1,300,1024]{2,1,0:T(8,128)S(1)} %get-tuple-element.12), kind=kLoop, calls=%fused_computation.47 | loop fusion | flops 921600 | bytes 7372800 | tf_op jit(solution)/shard_map/sub | solution.py:45
  293.0 10.4 %reduce-scatter.4.cloned.1.call-done = bf16[1,300,1024]{2,1,0:T(8,128)(2,1)} async-done(((bf16[16,300,1024]{2,1,0:T(8,128)(2,1)}), bf16[1,300,1024]{2,1,0:T(8,128)(2,1)}) %reduce-scatter.4.cloned.1.call-update) | async-done | bytes 614416
  303.4 0.0 copy-done.1
  303.4 2.2 fusion.26
  305.5 2.3 copy.20
  307.8 2.3 copy.21
  (11 shorter events, 0.0 us)
Async XLA Ops:
  14.6 7.4 %copy-start = (f32[1,300,1024]{2,0,1:T(1,128)S(1)}, f32[1,300,1024]{2,0,1:T(1,128)}, u32[]{:S(2)}) copy-start(f32[1,300,1024]{2,0,1:T(1,128)} %param.8) | copy-start | bytes 3686404
  14.6 8.7 %copy-start.5 = (s32[3]{0:T(128)S(1)}, s32[3]{0:T(128)}, u32[]{:S(2)}) copy-start(s32[3]{0:T(128)} %param.13) | copy-start | bytes 40
  14.6 17.1 %copy-start.6 = (s32[3]{0:T(128)S(1)}, s32[3]{0:T(128)}, u32[]{:S(2)}) copy-start(s32[3]{0:T(128)} %param.14) | copy-start | bytes 40
  14.6 155.1 %all-to-all-start = ((bf16[16,1,300,1024]{3,2,1,0:T(8,128)(2,1)}), bf16[16,1,300,1024]{3,2,1,0:T(8,128)(2,1)}, u32[]{:S(2)}, u32[]{:S(2)}) async-start(bf16[16,1,300,1024]{3,2,1,0:T(8,128)(2,1)} %stack.2), calls=%async_computation | async-start | bytes 19922944 | tf_op jit(solution)/shard_map/all_to_all | solution.py:62
  22.0 41.2 %all-gather.2.cloned.1.call-start = ((), (), s32[]{:S(2)}) async-start(), calls=%async_computation.3 | async-start | bytes 5603328 | tf_op jit(solution)/shard_map/all_gather | solution.py:56
  23.0 280.3 %reduce-scatter.4.cloned.1.call-start = ((), (), s32[]{:S(2)}) async-start(), calls=%async_computation.4 | async-start | bytes 10584064
  169.7 21.9 %slice-start.5 = ((s8[12582912]{0:T(1024)(128)(4,1)}), s8[4194304]{0:T(1024)(128)(4,1)S(1)}, s32[]{:S(2)}) async-start(s8[12582912]{0:T(1024)(128)(4,1)} %bitcast.139), calls=%async_computation.10 | async-start | bytes 8388608
  169.7 21.9 %slice-start.6 = ((s8[12582912]{0:T(1024)(128)(4,1)}), s8[4194304]{0:T(1024)(128)(4,1)S(1)}, s32[]{:S(2)}) async-start(s8[12582912]{0:T(1024)(128)(4,1)} %bitcast.139), calls=%async_computation.11 | async-start | bytes 8388608
  177.9 9.3 %copy-start.7 = (bf16[1024,1024]{1,0:T(8,128)(2,1)S(1)}, bf16[1024,1024]{1,0:T(8,128)(2,1)}, u32[]{:S(2)}) copy-start(bf16[1024,1024]{1,0:T(8,128)(2,1)} %fusion.14) | copy-start | bytes 6291460
  177.9 13.8 %slice-start.7 = ((s8[12582912]{0:T(1024)(128)(4,1)}), s8[4194304]{0:T(1024)(128)(4,1)S(1)}, s32[]{:S(2)}) async-start(s8[12582912]{0:T(1024)(128)(4,1)} %bitcast.139), calls=%async_computation.12 | async-start | bytes 8388608
  190.1 7.2 %slice-start = ((s8[19922944]{0:T(1024)(128)(4,1)}), s8[4194304]{0:T(1024)(128)(4,1)S(1)}, s32[]{:S(2)}) async-start(s8[19922944]{0:T(1024)(128)(4,1)} %bitcast.136), calls=%async_computation.5 | async-start | bytes 8388608
  191.7 5.6 %slice-start.1 = ((s8[19922944]{0:T(1024)(128)(4,1)}), s8[4194304]{0:T(1024)(128)(4,1)S(1)}, s32[]{:S(2)}) async-start(s8[19922944]{0:T(1024)(128)(4,1)} %bitcast.136), calls=%async_computation.6 | async-start | bytes 8388608
  191.7 5.6 %slice-start.2 = ((s8[19922944]{0:T(1024)(128)(4,1)}), s8[4194304]{0:T(1024)(128)(4,1)S(1)}, s32[]{:S(2)}) async-start(s8[19922944]{0:T(1024)(128)(4,1)} %bitcast.136), calls=%async_computation.7 | async-start | bytes 8388608
  191.7 5.6 %slice-start.3 = ((s8[19922944]{0:T(1024)(128)(4,1)}), s8[4194304]{0:T(1024)(128)(4,1)S(1)}, s32[]{:S(2)}) async-start(s8[19922944]{0:T(1024)(128)(4,1)} %bitcast.136), calls=%async_computation.8 | async-start | bytes 8388608
  191.7 6.1 %slice-start.4 = ((s8[19922944]{0:T(1024)(128)(4,1)}), s8[3145728]{0:T(1024)(128)(4,1)S(1)}, s32[]{:S(2)}) async-start(s8[19922944]{0:T(1024)(128)(4,1)} %bitcast.136), calls=%async_computation.9 | async-start | bytes 6291456
  205.5 1.3 copy-start.2
  213.7 1.6 copy-start.8
  217.4 2.2 copy-start.3
  285.5 1.5 copy-start.4
  287.0 16.4 %copy-start.1 = (f32[1,300,1024]{2,0,1:T(1,128)S(1)}, f32[1,300,1024]{2,0,1:T(1,128)}, u32[]{:S(2)}) copy-start(f32[1,300,1024]{2,0,1:T(1,128)} %param.9) | copy-start | bytes 3686404
Sparse Core Ops, SparseCore 0:
  25.0 38.0 all-gather.1
  213.9 89.4 reduce-scatter.3
